TPU v7x, 256 devices: a whole 4x4x8 slice. The times are simulated.
256 devices in a mesh: seq: 32 (over z, y), head: 2 (over core), dp: 4 (over x).
Axes of the slice: x: 4, y: 4, z: 8, core: 2. Of those that a mesh axis runs over, the one named last changes fastest.
Arguments:
- queries: bfloat16 [90112, 2048], P(('dp', 'seq'), 'head'), parts along dimension 0, may hold values from -96 to 96
- out_grad: bfloat16 [90112, 2048], P(('dp', 'seq'), 'head'), parts along dimension 0, may hold values from -16 to 16
- encodings: bfloat16 [1280, 16, 2048], P(('dp', 'seq'), None, 'head'), parts along dimension 0, may hold values from -6 to 6
- key_weight: bfloat16 [2048, 2048], P(None, 'head'), may hold values from -0.125 to 0.125
- value_weight: bfloat16 [2048, 2048], P(None, 'head'), may hold values from -0.125 to 0.125
- neighbours: int32 [1408, 2], P(('dp', 'seq')), parts along dimension 0, may hold values from 0 to 319, as said below
Outputs:
- query_grad: bfloat16 [90112, 2048], P(('dp', 'seq'), 'head'), parts along dimension 0
- encoding_grad: bfloat16 [1280, 16, 2048], P(('dp', 'seq'), None, 'head'), parts along dimension 0
There are 4 independent parts, one for each index of `dp`. A program takes and returns all parts, laid end to end along the dimension named above; an argument that names none is the same for every part. Nothing has to cross between parts.
Inputs may be any that keep to these rules, and one draw needn't show every extreme that they name: `neighbours`: row r of encodings is held by index r // 10 of seq. In each aligned block of 11 spans, at most 2 of the 22 ids belong to one holder, and some holder has exactly 2. A span's two ids differ.
All inputs are finite; a program needn't handle non-finite values.
Results may differ from a plain program's by a relative error of at most 0.011.
Values may be sent and summed in bfloat16 or wider, within the bound.
No kernel may reach another device: no remote copies, remote signals or barrier semaphores. Data moves between devices by JAX's collectives and lax.ppermute only.
A program may use at most 64 MiB of HBM per device.

v0:
```python
import math
import jax
import jax.numpy as jnp
from jax import lax
from jax.sharding import PartitionSpec as P

D = 2048
HEADS = 16


def slot_ranks(owner_ids):
    count = owner_ids.shape[-1]
    same_owner = owner_ids[..., :, None] == owner_ids[..., None, :]
    positions = jnp.arange(count, dtype=jnp.int32)
    earlier = positions[None, :] < positions[:, None]
    return jnp.sum(same_owner & earlier, axis=-1)


def on_device(queries, out_grad, encodings, key_weight, value_weight, neighbours):
    seq_count = lax.axis_size("seq")
    seq_index = lax.axis_index("seq")
    spans_here = neighbours.shape[0]
    ref_count = 2 * spans_here
    rows_here, neighbour_len, half_width = encodings.shape
    full_width = key_weight.shape[0]
    tok_rows = queries.shape[0]
    span_len = tok_rows // spans_here
    head_size = D // HEADS
    heads_here = half_width // head_size
    scaling = 1.0 / math.sqrt(head_size)
    capacity = max(2, ref_count // seq_count)
    slot_count = seq_count * capacity
    all_lists = lax.all_gather(neighbours, "seq", axis=0, tiled=True).reshape(seq_count, ref_count)
    owner_table = all_lists // rows_here
    local_table = all_lists % rows_here
    rank_table = slot_ranks(owner_table)
    own_ids = neighbours.reshape(ref_count)
    own_owner = own_ids // rows_here
    position = own_owner * capacity + slot_ranks(own_owner)
    slot_ids = jnp.arange(capacity, dtype=jnp.int32)
    chosen = (owner_table == seq_index)[:, None, :] & (
        rank_table[:, None, :] == slot_ids[None, :, None]
    )
    filled = jnp.any(chosen, axis=-1)
    slot_row = jnp.sum(jnp.where(chosen, local_table[:, None, :], 0), axis=-1)
    select = filled[..., None] & (
        slot_row[..., None] == jnp.arange(rows_here, dtype=jnp.int32)[None, None, :]
    )
    select = select.astype(jnp.bfloat16).reshape(slot_count, rows_here)
    flat_enc = encodings.reshape(rows_here, neighbour_len * half_width)
    outgoing = jnp.dot(select, flat_enc, preferred_element_type=jnp.float32).astype(jnp.bfloat16)
    outgoing = outgoing.reshape(seq_count, capacity, neighbour_len, half_width)
    arrived = lax.all_to_all(outgoing, "seq", split_axis=0, concat_axis=0, tiled=True)
    flat_arrived = arrived.reshape(slot_count, neighbour_len, half_width)
    whole = lax.all_gather(flat_arrived, "head", axis=2, tiled=True)
    full_rows = jnp.take(whole, position, axis=0)
    flat_rows = full_rows.reshape(ref_count * neighbour_len, full_width)
    keys = jnp.dot(flat_rows, key_weight, preferred_element_type=jnp.float32).astype(jnp.bfloat16)
    values = jnp.dot(flat_rows, value_weight, preferred_element_type=jnp.float32).astype(
        jnp.bfloat16
    )
    query_heads = queries.reshape(spans_here, span_len, heads_here, head_size)
    grad_heads = out_grad.reshape(spans_here, span_len, heads_here, head_size)
    key_heads = keys.reshape(spans_here, 2 * neighbour_len, heads_here, head_size)
    value_heads = values.reshape(spans_here, 2 * neighbour_len, heads_here, head_size)
    scores = (
        jnp.einsum("cthd,cuhd->chtu", query_heads, key_heads, preferred_element_type=jnp.float32)
        * scaling
    )
    scores = scores - jnp.max(scores, axis=-1, keepdims=True)
    raised = jnp.exp(scores)
    probs = raised / jnp.sum(raised, axis=-1, keepdims=True)
    probs_b = probs.astype(jnp.bfloat16)
    attended = jnp.einsum(
        "chtu,cuhd->cthd", probs_b, value_heads, preferred_element_type=jnp.float32
    )
    delta = jnp.transpose(jnp.sum(grad_heads.astype(jnp.float32) * attended, axis=-1), (0, 2, 1))
    dprobs = jnp.einsum(
        "cthd,cuhd->chtu", grad_heads, value_heads, preferred_element_type=jnp.float32
    )
    dscores = (probs * (dprobs - delta[..., None])).astype(jnp.bfloat16)
    query_grad = (
        jnp.einsum("chtu,cuhd->cthd", dscores, key_heads, preferred_element_type=jnp.float32)
        * scaling
    )
    query_grad = query_grad.astype(jnp.bfloat16).reshape(tok_rows, half_width)
    key_grad = (
        jnp.einsum("chtu,cthd->cuhd", dscores, query_heads, preferred_element_type=jnp.float32)
        * scaling
    )
    key_grad = key_grad.astype(jnp.bfloat16).reshape(ref_count * neighbour_len, half_width)
    value_grad = jnp.einsum(
        "chtu,cthd->cuhd", probs_b, grad_heads, preferred_element_type=jnp.float32
    )
    value_grad = value_grad.astype(jnp.bfloat16).reshape(ref_count * neighbour_len, half_width)
    contract = (((1,), (1,)), ((), ()))
    partial_value = lax.dot_general(
        key_grad, key_weight, contract, preferred_element_type=jnp.float32
    )
    partial_value = partial_value + lax.dot_general(
        value_grad, value_weight, contract, preferred_element_type=jnp.float32
    )
    summed = lax.psum_scatter(
        partial_value.reshape(ref_count, neighbour_len, full_width),
        "head",
        scatter_dimension=2,
        tiled=True,
    )
    ref_grad = summed.astype(jnp.bfloat16)
    returning = (
        jnp.zeros((slot_count, neighbour_len, half_width), jnp.bfloat16).at[position].set(ref_grad)
    )
    returning = returning.reshape(seq_count, capacity, neighbour_len, half_width)
    came_back = lax.all_to_all(returning, "seq", split_axis=0, concat_axis=0, tiled=True).reshape(
        slot_count, neighbour_len * half_width
    )
    encoding_grad = lax.dot_general(
        select, came_back, (((0,), (0,)), ((), ())), preferred_element_type=jnp.float32
    )
    encoding_grad = encoding_grad.astype(jnp.bfloat16).reshape(rows_here, neighbour_len, half_width)
    return (query_grad, encoding_grad)


def solution(mesh):
    return jax.shard_map(
        on_device,
        mesh=mesh,
        in_specs=(
            P(("dp", "seq"), "head"),
            P(("dp", "seq"), "head"),
            P(("dp", "seq"), None, "head"),
            P(None, "head"),
            P(None, "head"),
            P(("dp", "seq"), None),
        ),
        out_specs=(P(("dp", "seq"), "head"), P(("dp", "seq"), None, "head")),
        check_vma=False,
    )
```

profile of v0, /device:TPU:2, one launch (start us, length us, event | category | flops | bytes accessed | tf_op | source)
XLA Modules:
  0.0 242.0 jit_solution(4702923652695932510)
XLA Ops:
  7.2 46.3 %all-gather = s32[32,11,2]{1,2,0:T(2,128)S(1)} all-gather(s32[1,11,2]{1,2,0:T(2,128)} %bitcast.115), channel_id=1, replica_groups=mesh['seq'=32,'head'=2,'dp'=4] {'seq'}, dimensions={0}, use_global_device_ids=true | all-gather | bytes 2904 | tf_op jit(solution)/shard_map/all_gather | solution.py:33
  54.4 1.0 pad.1
  55.8 0.7 convolution_convert_fusion
  56.5 1.2 copy.110
  57.7 46.8 %all_to_all.10 = bf16[32,2,16,1024]{3,2,1,0:T(8,128)(2,1)} all-to-all(bf16[32,2,16,1024]{3,2,1,0:T(8,128)(2,1)S(1)} %bitcast.94), channel_id=1, replica_groups=mesh['seq'=32,'head'=2,'dp'=4] {'seq'}, dimensions={0} | all-to-all | bytes 4194304 | tf_op jit(solution)/shard_map/all_to_all | solution.py:53
  106.6 0.9 copy-done.1
  107.6 1.5 copy.114
  109.1 11.6 %all-gather.3.cloned.1.call-done = bf16[64,16,2048]{2,1,0:T(8,128)(2,1)} async-done(((bf16[64,16,1024]{2,1,0:T(8,128)(2,1)}), bf16[64,16,2048]{2,1,0:T(8,128)(2,1)}) %all-gather.3.cloned.1.call-update) | async-done | bytes 4194320 | tf_op jit(solution)/shard_map/all_gather | solution.py:55
  120.7 2.8 %gather_fusion = bf16[22,16,2048]{2,1,0:T(8,128)(2,1)S(1)} fusion(bf16[64,16,2048]{2,1,0:T(8,128)(2,1)} %all-gather.3.cloned.1.call-done, s32[1024]{0:T(1024)S(1)} %pad_clamp_fusion), kind=kCustom, calls=%fused_computation | custom fusion | bytes 2883672 | tf_op jit(solution)/shard_map/jit(_take)/gather | solution.py:56
  123.8 4.4 %fusion.10 = bf16[44,8,8,128]{3,1,2,0:T(8,128)(2,1)S(1)} fusion(bf16[352,2048]{1,0:T(8,128)(2,1)S(1)} %bitcast_select_fusion, bf16[2048,1024]{1,0:T(8,128)(2,1)} %param.9), kind=kOutput, calls=%fused_computation.25 | convolution fusion | flops 1476755456 | bytes 6356992 | tf_op jit(solution)/shard_map/dot_general | solution.py:58
  128.4 2.0 fusion.41
  130.4 2.4 %fusion.13 = bf16[11,32,8,128]{3,1,2,0:T(8,128)(2,1)S(1)} fusion(bf16[11,64,8,128]{3,2,1,0:T(8,128)(2,1)} %bitcast.106, f32[11,8,64,32]{2,3,1,0:T(8,128)} %get-tuple-element.7, f32[11,8,64]{2,1,0:T(8,128)S(1)} %get-tuple-element.6), kind=kOutput, calls=%fused_computation.28 | convolution fusion | flops 46858240 | bytes 2906112 | tf_op jit(solution)/shard_map/chtu,cthd->cuhd/dot_general | solution.py:92
  133.4 0.9 copy-done.4
  134.3 1.7 fusion.11
  136.2 1.2 copy-done.2
  137.4 1.3 fusion.1
  138.7 0.9 fusion.9
  140.3 1.4 copy-done.6
  141.7 1.7 fusion.20
  143.4 3.3 %convolution_add_fusion = f32[352,2048]{1,0:T(8,128)} fusion(f32[352,2048]{1,0:T(8,128)S(1)} %fusion.20, bf16[2048,1024]{1,0:T(8,128)(2,1)S(1)} %copy-done.7, bf16[44,8,8,128]{3,2,1,0:T(8,128)(2,1)S(1)} %bitcast.111), kind=kOutput, calls=%fused_computation.8 | convolution fusion | flops 1477115904 | bytes 10682368 | tf_op jit(solution)/shard_map/dot_general | solution.py:100
  146.8 17.5 %reduce-scatter.2.cloned.1.call-done = f32[22,16,1024]{2,1,0:T(8,128)} async-done(((f32[22,16,2048]{2,1,0:T(8,128)}), f32[22,16,1024]{2,1,0:T(8,128)}) %reduce-scatter.2.cloned.1.call-update) | async-done | bytes 1441808 | tf_op jit(solution)/shard_map/reduce_scatter | solution.py:103
  164.3 1.4 convert_element_type.63
  165.7 1.6 broadcast_in_dim.34
  167.4 4.6 %scatter_fusion = bf16[64,16,1024]{2,1,0:T(8,128)(2,1)} fusion(bf16[64,16,1024]{2,1,0:T(8,128)(2,1)} %broadcast_in_dim.34, s32[22]{0:T(128)S(1)} %fusion.38, bf16[22,16,1024]{2,1,0:T(8,128)(2,1)S(1)} %convert_element_type.63), kind=kCustom, calls=%fused_computation.1 | custom fusion | bytes 2162776 | tf_op jit(solution)/shard_map/scatter | solution.py:111
  171.9 9.9 %all-to-all-start.1 = ((bf16[32,2,16,1024]{3,2,1,0:T(8,128)(2,1)}), bf16[32,2,16,1024]{3,2,1,0:T(8,128)(2,1)S(1)}, u32[]{:S(2)}, u32[]{:S(2)}) async-start(bf16[32,2,16,1024]{3,2,1,0:T(8,128)(2,1)} %bitcast.13), calls=%async_computation.2 | async-start | bytes 4194304 | tf_op jit(solution)/shard_map/all_to_all | solution.py:114
  181.9 0.6 fusion.7
  182.5 1.1 copy.103
  183.6 1.5 copy.150
  185.1 47.2 %all-to-all-done.1 = bf16[32,2,16,1024]{3,2,1,0:T(8,128)(2,1)S(1)} async-done(((bf16[32,2,16,1024]{3,2,1,0:T(8,128)(2,1)}), bf16[32,2,16,1024]{3,2,1,0:T(8,128)(2,1)S(1)}, u32[]{:S(2)}, u32[]{:S(2)}) %all-to-all-start.1) | async-done | bytes 2097184 | tf_op jit(solution)/shard_map/all_to_all | solution.py:114
  232.3 1.2 copy.118
  233.5 0.5 convolution_convert_fusion.1
  234.4 0.8 slice.2
  (58 shorter events, 5.5 us)
Async XLA Ops:
  7.2 113.5 %all-gather.3.cloned.1.call-start = ((), (), s32[]{:S(2)}) async-start(), calls=%async_computation.3 | async-start | bytes 6291456 | tf_op jit(solution)/shard_map/all_gather | solution.py:55
  104.5 0.7 copy-start.5
  104.5 1.6 copy-start
  104.6 59.7 %reduce-scatter.2.cloned.1.call-start = ((), (), s32[]{:S(2)}) async-start(), calls=%async_computation.4 | async-start | bytes 4325376 | tf_op jit(solution)/shard_map/reduce_scatter | solution.py:103
  106.2 1.4 copy-start.1
  123.8 4.4 %copy-start.3 = (bf16[352,2048]{1,0:T(8,128)(2,1)}, bf16[352,2048]{1,0:T(8,128)(2,1)S(1)}, u32[]{:S(2)}) copy-start(bf16[352,2048]{1,0:T(8,128)(2,1)S(1)} %bitcast_select_fusion) | copy-start | bytes 4325380
  130.4 3.1 %copy-start.7 = (bf16[2048,1024]{1,0:T(8,128)(2,1)S(1)}, bf16[2048,1024]{1,0:T(8,128)(2,1)}, u32[]{:S(2)}) copy-start(bf16[2048,1024]{1,0:T(8,128)(2,1)} %param.10) | copy-start | bytes 12582916
  132.8 1.5 copy-start.4
  134.3 1.9 copy-start.8
  136.0 1.4 copy-start.2
  139.5 2.2 copy-start.6
  171.9 60.4 %all-to-all-start.1 = ((bf16[32,2,16,1024]{3,2,1,0:T(8,128)(2,1)}), bf16[32,2,16,1024]{3,2,1,0:T(8,128)(2,1)S(1)}, u32[]{:S(2)}, u32[]{:S(2)}) async-start(bf16[32,2,16,1024]{3,2,1,0:T(8,128)(2,1)} %bitcast.13), calls=%async_computation.2 | async-start | bytes 4194304 | tf_op jit(solution)/shard_map/all_to_all | solution.py:114
Sparse Core Ops, SparseCore 0:
  104.7 15.9 all-gather.2
  146.9 17.3 reduce-scatter.1
where the time goes:
time: 243 us; the launch traced here: 242 us
  blocking collectives  93.1 us (38%)
  waiting for transfers between devices  76.3 us (31%)
  local copies, waits for them, and re-layouts  25.6 us (11%)
  matrix products  20 us (8%)
  between operations  14.4 us (6%)
  starting transfers between devices  10.2 us (4%)
    all_to_all x1, waiting for transfers between devices, on_device(): lax.all_to_all(returning, 'seq', split_axis=0, concat_axis=0, tiled=True)  47.2 us
    all_to_all x1, blocking collectives, on_device(): lax.all_to_all(outgoing, 'seq', split_axis=0, concat_axis=0, tiled=True)  46.8 us
    all_gather x1, blocking collectives, on_device(): lax.all_gather(neighbours, 'seq', axis=0, tiled=True)  46.3 us
    reduce_scatter x1, waiting for transfers between devices, on_device(): lax.psum_scatter(partial_value.reshape(ref_count, neighbour_len, full_wid...  17.5 us
    unnamed x28, local copies, waits for them, and re-layouts  12.9 us
    all_gather x1, waiting for transfers between devices, on_device(): whole = lax.all_gather(flat_arrived, 'head', axis=2, tiled=True)  11.6 us
    all_to_all x1, starting transfers between devices, on_device(): lax.all_to_all(returning, 'seq', split_axis=0, concat_axis=0, tiled=True)  9.91 us
  transfers between devices with their start and end apart: 3, of which 3 were waited for; matrix products, arithmetic and copies ran while one was open for 3% of the time, Pallas kernels for 0%

commit v1 on v0

--- a/solution.py
+++ b/solution.py
@@ -30,7 +30,9 @@
     scaling = 1.0 / math.sqrt(head_size)
     capacity = max(2, ref_count // seq_count)
     slot_count = seq_count * capacity
-    all_lists = lax.all_gather(neighbours, "seq", axis=0, tiled=True).reshape(seq_count, ref_count)
+    all_lists = jnp.concatenate(
+        lax.all_to_all(jnp.stack([neighbours] * lax.axis_size("seq")), "seq", 0, 0), axis=0
+    ).reshape(seq_count, ref_count)
     owner_table = all_lists // rows_here
     local_table = all_lists % rows_here
     rank_table = slot_ranks(owner_table)

time: 243 us -> 224 us (0.922)
  blocking collectives: 93.1 us -> 53.4 us
  starting transfers between devices: 10.2 us -> 21.7 us
  waiting for transfers between devices: 76.3 us -> 84.6 us
    all_gather x1 -> x0, blocking collectives: 46.3 us -> none  [on_device(): lax.all_gather(neighbours, 'seq', axis=0, tiled=True)]
    all_to_all x0 -> x1, starting transfers between devices: none -> 11.5 us  [on_device(): lax.all_to_all(jnp.stack([neighbours] * lax.axis_size('seq')), 'seq', 0, 0)]
    all_to_all x0 -> x1, waiting for transfers between devices: none -> 8.46 us  [on_device(): lax.all_to_all(jnp.stack([neighbours] * lax.axis_size('seq')), 'seq', 0, 0)]
    all_to_all x1, blocking collectives: 46.8 us -> 53.4 us  [on_device(): lax.all_to_all(outgoing, 'seq', split_axis=0, concat_axis=0, tiled=True)]
  transfers between devices with their start and end apart: 3 -> 4, of which waited for: 3 -> 4; matrix products, arithmetic and copies ran while one was open for 3% -> 3% of each run, Pallas kernels for 0% -> 0%
where the time goes in v1:
time: 224 us; the launch traced here: 223 us
  waiting for transfers between devices  84.6 us (38%)
  blocking collectives  53.4 us (24%)
  local copies, waits for them, and re-layouts  26.9 us (12%)
  starting transfers between devices  21.7 us (10%)
  matrix products  20 us (9%)
  between operations  14.4 us (6%)
  other arithmetic  2.26 us (1%)
    all_to_all x1, blocking collectives, on_device(): lax.all_to_all(outgoing, 'seq', split_axis=0, concat_axis=0, tiled=True)  53.4 us
    all_to_all x1, waiting for transfers between devices, on_device(): lax.all_to_all(returning, 'seq', split_axis=0, concat_axis=0, tiled=True)  47.2 us
    reduce_scatter x1, waiting for transfers between devices, on_device(): lax.psum_scatter(partial_value.reshape(ref_count, neighbour_len, full_wid...  17.5 us
    unnamed x28, local copies, waits for them, and re-layouts  12.9 us
    all_to_all x1, starting transfers between devices, on_device(): lax.all_to_all(jnp.stack([neighbours] * lax.axis_size('seq')), 'seq', 0, 0)  11.5 us
    all_gather x1, waiting for transfers between devices, on_device(): whole = lax.all_gather(flat_arrived, 'head', axis=2, tiled=True)  11.3 us
    all_to_all x1, starting transfers between devices, on_device(): lax.all_to_all(returning, 'seq', split_axis=0, concat_axis=0, tiled=True)  9.91 us
    all_to_all x1, waiting for transfers between devices, on_device(): lax.all_to_all(jnp.stack([neighbours] * lax.axis_size('seq')), 'seq', 0, 0)  8.46 us
  transfers between devices with their start and end apart: 4, of which 4 were waited for; matrix products, arithmetic and copies ran while one was open for 3% of the time, Pallas kernels for 0%

profile of v1, /device:TPU:2, one launch (start us, length us, event | category | flops | bytes accessed | tf_op | source)
XLA Modules:
  0.0 223.3 jit_solution(3722127002867488645)
XLA Ops:
  7.2 1.3 stack.2
  8.5 11.5 %all-to-all-start = ((s32[32,11,2]{1,2,0:T(2,128)}), s32[32,11,2]{1,2,0:T(2,128)S(1)}, u32[]{:S(2)}, u32[]{:S(2)}) async-start(s32[32,11,2]{1,2,0:T(2,128)} %stack.2), calls=%async_computation | async-start | bytes 65536 | tf_op jit(solution)/shard_map/all_to_all | solution.py:34
  20.0 1.0 pad.1
  21.3 8.5 %all-to-all-done = s32[32,11,2]{1,2,0:T(2,128)S(1)} async-done(((s32[32,11,2]{1,2,0:T(2,128)}), s32[32,11,2]{1,2,0:T(2,128)S(1)}, u32[]{:S(2)}, u32[]{:S(2)}) %all-to-all-start) | async-done | bytes 2848 | tf_op jit(solution)/shard_map/all_to_all | solution.py:34
  30.7 0.7 convolution_convert_fusion
  31.5 1.2 copy.133
  32.7 53.4 %all_to_all.15 = bf16[32,2,16,1024]{3,2,1,0:T(8,128)(2,1)} all-to-all(bf16[32,2,16,1024]{3,2,1,0:T(8,128)(2,1)S(1)} %bitcast.93), channel_id=1, replica_groups=mesh['seq'=32,'head'=2,'dp'=4] {'seq'}, dimensions={0} | all-to-all | bytes 4194304 | tf_op jit(solution)/shard_map/all_to_all | solution.py:55
  88.1 0.9 copy-done.1
  89.1 1.5 copy.137
  90.6 11.3 %all-gather.2.cloned.1.call-done = bf16[64,16,2048]{2,1,0:T(8,128)(2,1)} async-done(((bf16[64,16,1024]{2,1,0:T(8,128)(2,1)}), bf16[64,16,2048]{2,1,0:T(8,128)(2,1)}) %all-gather.2.cloned.1.call-update) | async-done | bytes 4194320 | tf_op jit(solution)/shard_map/all_gather | solution.py:57
  102.0 2.8 %gather_fusion = bf16[22,16,2048]{2,1,0:T(8,128)(2,1)S(1)} fusion(bf16[64,16,2048]{2,1,0:T(8,128)(2,1)} %all-gather.2.cloned.1.call-done, s32[1024]{0:T(1024)S(1)} %pad_clamp_fusion), kind=kCustom, calls=%fused_computation | custom fusion | bytes 2883672 | tf_op jit(solution)/shard_map/jit(_take)/gather | solution.py:58
  105.1 4.4 %fusion.10 = bf16[44,8,8,128]{3,1,2,0:T(8,128)(2,1)S(1)} fusion(bf16[352,2048]{1,0:T(8,128)(2,1)S(1)} %bitcast_select_fusion, bf16[2048,1024]{1,0:T(8,128)(2,1)} %param.9), kind=kOutput, calls=%fused_computation.25 | convolution fusion | flops 1476755456 | bytes 6356992 | tf_op jit(solution)/shard_map/dot_general | solution.py:60
  109.7 2.0 fusion.41
  111.7 2.4 %fusion.13 = bf16[11,32,8,128]{3,1,2,0:T(8,128)(2,1)S(1)} fusion(bf16[11,64,8,128]{3,2,1,0:T(8,128)(2,1)} %bitcast.105, f32[11,8,64,32]{2,3,1,0:T(8,128)} %get-tuple-element.7, f32[11,8,64]{2,1,0:T(8,128)S(1)} %get-tuple-element.6), kind=kOutput, calls=%fused_computation.28 | convolution fusion | flops 46858240 | bytes 2906112 | tf_op jit(solution)/shard_map/chtu,cthd->cuhd/dot_general | solution.py:94
  114.7 0.9 copy-done.4
  115.6 1.7 fusion.11
  117.5 1.2 copy-done.2
  118.7 1.3 fusion.1
  120.0 0.9 fusion.9
  121.6 1.4 copy-done.6
  123.0 1.7 fusion.20
  124.7 3.3 %convolution_add_fusion = f32[352,2048]{1,0:T(8,128)} fusion(f32[352,2048]{1,0:T(8,128)S(1)} %fusion.20, bf16[2048,1024]{1,0:T(8,128)(2,1)S(1)} %copy-done.7, bf16[44,8,8,128]{3,2,1,0:T(8,128)(2,1)S(1)} %bitcast.110), kind=kOutput, calls=%fused_computation.8 | convolution fusion | flops 1477115904 | bytes 10682368 | tf_op jit(solution)/shard_map/dot_general | solution.py:102
  128.1 17.5 %reduce-scatter.2.cloned.1.call-done = f32[22,16,1024]{2,1,0:T(8,128)} async-done(((f32[22,16,2048]{2,1,0:T(8,128)}), f32[22,16,1024]{2,1,0:T(8,128)}) %reduce-scatter.2.cloned.1.call-update) | async-done | bytes 1441808 | tf_op jit(solution)/shard_map/reduce_scatter | solution.py:105
  145.6 1.4 convert_element_type.63
  147.0 1.6 broadcast_in_dim.34
  148.6 4.6 %scatter_fusion = bf16[64,16,1024]{2,1,0:T(8,128)(2,1)} fusion(bf16[64,16,1024]{2,1,0:T(8,128)(2,1)} %broadcast_in_dim.34, s32[22]{0:T(128)S(1)} %fusion.38, bf16[22,16,1024]{2,1,0:T(8,128)(2,1)S(1)} %convert_element_type.63), kind=kCustom, calls=%fused_computation.1 | custom fusion | bytes 2162776 | tf_op jit(solution)/shard_map/scatter | solution.py:113
  153.2 9.9 %all-to-all-start.2 = ((bf16[32,2,16,1024]{3,2,1,0:T(8,128)(2,1)}), bf16[32,2,16,1024]{3,2,1,0:T(8,128)(2,1)S(1)}, u32[]{:S(2)}, u32[]{:S(2)}) async-start(bf16[32,2,16,1024]{3,2,1,0:T(8,128)(2,1)} %bitcast.12), calls=%async_computation.3 | async-start | bytes 4194304 | tf_op jit(solution)/shard_map/all_to_all | solution.py:116
  163.8 1.1 copy.126
  164.9 1.5 copy.173
  166.4 47.2 %all-to-all-done.2 = bf16[32,2,16,1024]{3,2,1,0:T(8,128)(2,1)S(1)} async-done(((bf16[32,2,16,1024]{3,2,1,0:T(8,128)(2,1)}), bf16[32,2,16,1024]{3,2,1,0:T(8,128)(2,1)S(1)}, u32[]{:S(2)}, u32[]{:S(2)}) %all-to-all-start.2) | async-done | bytes 2097184 | tf_op jit(solution)/shard_map/all_to_all | solution.py:116
  213.6 1.2 copy.141
  215.7 0.8 slice.2
  (60 shorter events, 6.6 us)
Async XLA Ops:
  8.5 21.3 %all-to-all-start = ((s32[32,11,2]{1,2,0:T(2,128)}), s32[32,11,2]{1,2,0:T(2,128)S(1)}, u32[]{:S(2)}, u32[]{:S(2)}) async-start(s32[32,11,2]{1,2,0:T(2,128)} %stack.2), calls=%async_computation | async-start | bytes 65536 | tf_op jit(solution)/shard_map/all_to_all | solution.py:34
  20.0 82.0 %all-gather.2.cloned.1.call-start = ((), (), s32[]{:S(2)}) async-start(), calls=%async_computation.4 | async-start | bytes 6291456 | tf_op jit(solution)/shard_map/all_gather | solution.py:57
  86.1 0.7 copy-start.5
  86.1 1.6 copy-start
  86.1 59.5 %reduce-scatter.2.cloned.1.call-start = ((), (), s32[]{:S(2)}) async-start(), calls=%async_computation.5 | async-start | bytes 4325376 | tf_op jit(solution)/shard_map/reduce_scatter | solution.py:105
  87.7 1.4 copy-start.1
  105.1 4.4 %copy-start.3 = (bf16[352,2048]{1,0:T(8,128)(2,1)}, bf16[352,2048]{1,0:T(8,128)(2,1)S(1)}, u32[]{:S(2)}) copy-start(bf16[352,2048]{1,0:T(8,128)(2,1)S(1)} %bitcast_select_fusion) | copy-start | bytes 4325380
  111.7 3.1 %copy-start.7 = (bf16[2048,1024]{1,0:T(8,128)(2,1)S(1)}, bf16[2048,1024]{1,0:T(8,128)(2,1)}, u32[]{:S(2)}) copy-start(bf16[2048,1024]{1,0:T(8,128)(2,1)} %param.10) | copy-start | bytes 12582916
  114.1 1.5 copy-start.4
  115.6 1.9 copy-start.8
  117.3 1.4 copy-start.2
  120.8 2.2 copy-start.6
  153.2 60.4 %all-to-all-start.2 = ((bf16[32,2,16,1024]{3,2,1,0:T(8,128)(2,1)}), bf16[32,2,16,1024]{3,2,1,0:T(8,128)(2,1)S(1)}, u32[]{:S(2)}, u32[]{:S(2)}) async-start(bf16[32,2,16,1024]{3,2,1,0:T(8,128)(2,1)} %bitcast.12), calls=%async_computation.3 | async-start | bytes 4194304 | tf_op jit(solution)/shard_map/all_to_all | solution.py:116
Sparse Core Ops, SparseCore 0:
  86.2 15.6 all-gather.1
  128.2 17.3 reduce-scatter.1
